TPU v7x, 32 devices: a whole 2x2x4 slice. The times are simulated.
32 devices in a mesh: shard: 2 (over x), ctx: 4 (over y, core), tp: 4 (over z).
Axes of the slice: x: 2, y: 2, z: 4, core: 2. Of those that a mesh axis runs over, the one named last changes fastest.
Arguments:
- inputs: bfloat16 [2, 2, 4096, 768], P('shard', None, 'ctx'), may hold values from -6 to 6
- lengths: int32 [2, 2], P('shard'), may hold values from 2048 to 4096, as said below
- attn_gain: bfloat16 [768], P('shard'), may hold values from 0.099609375 to 1.8984375
- mlp_gain: bfloat16 [768], P('shard'), may hold values from 0.099609375 to 1.8984375
- qkv_weight: bfloat16 [768, 3, 768], P('shard', None, 'tp'), may hold values from -0.21875 to 0.21875
- attn_weight: bfloat16 [768, 768], P('tp', 'shard'), may hold values from -0.875 to 0.875
- mlp_in_weight: bfloat16 [768, 2, 1152], P('shard', None, 'tp'), may hold values from -0.21875 to 0.21875
- mlp_out_weight: bfloat16 [1152, 768], P('tp', 'shard'), may hold values from -0.1875 to 0.1875
- cotangent: bfloat16 [2, 2, 4096, 768], P('shard', None, 'ctx'), may hold values from -6 to 6
Outputs:
- layer_out: bfloat16 [2, 2, 4096, 768], P('shard', None, 'ctx')
- input_grad: bfloat16 [2, 2, 4096, 768], P('shard', None, 'ctx')
- qkv_grad: float32 [768, 3, 768], P('shard', None, 'tp')
- attn_grad: float32 [768, 768], P('tp', 'shard')
- mlp_in_grad: float32 [768, 2, 1152], P('shard', None, 'tp')
- mlp_out_grad: float32 [1152, 768], P('tp', 'shard')
- attn_gain_grad: float32 [768], P(('shard', 'tp'))
- mlp_gain_grad: float32 [768], P(('shard', 'tp'))
Inputs may be any that keep to these rules, and one draw needn't show every extreme that they name: `lengths`: among the 2 sequences of each index of shard one has length 4096; some sequence has length 2048.
All inputs are finite; a program needn't handle non-finite values.
Results may differ from a plain program's by a relative error of at most 0.017.
Values may be sent and summed in bfloat16 or wider, within the bound.
A program may use at most 192 MiB of HBM per device.

v0:
```python
import math
import jax
import jax.numpy as jnp
from jax import lax
from jax.sharding import PartitionSpec as P

HD = 64
HALF = 64
norm_eps = 1e-05
rope_base = 10000.0
masked_score = -1e30


def padded(cells, sides, width):
    for axis, dim in sides:
        count = lax.axis_size(axis)
        ends = count - 1
        head = lax.slice_in_dim(cells, 0, width, axis=dim)
        tail = lax.slice_in_dim(cells, cells.shape[dim] - width, cells.shape[dim], axis=dim)
        cells = jnp.concatenate(
            [
                lax.ppermute(tail, axis, [(i, (i + 1) % count) for i in range(ends)]),
                cells,
                lax.ppermute(head, axis, [((i + 1) % count, i) for i in range(ends)]),
            ],
            axis=dim,
        )
    return cells


def layer_norm(values, gain_row):
    center = values - jnp.mean(values, axis=-1, keepdims=True)
    variance = jnp.mean(center * center, axis=-1, keepdims=True)
    return center * lax.rsqrt(variance + norm_eps) * gain_row


def rope_tables(positions):
    exponents = jnp.arange(0, HD, 2).astype(jnp.float32) / HD
    inverse = jnp.power(rope_base, -exponents)
    angles = positions[:, None] * inverse[None, :]
    angles = jnp.concatenate([angles, angles], axis=-1)[:, None, :]
    return (jnp.cos(angles), jnp.sin(angles))


def rotate(vector, cosine, sine_table):
    half_size = vector.shape[-1] // 2
    turned = jnp.concatenate([-vector[..., half_size:], vector[..., :half_size]], axis=-1)
    return vector * cosine + turned * sine_table


def geglu(gate_up):
    return jax.nn.gelu(gate_up[..., 0, :], approximate=False) * gate_up[..., 1, :]


def on_device(
    inputs,
    lengths,
    attn_gain,
    mlp_gain,
    qkv_weight,
    attn_weight,
    mlp_in_weight,
    mlp_out_weight,
    cotangent,
):
    gathered = (
        lax.all_gather(qkv_weight, "shard", axis=0, tiled=True),
        lax.all_gather(attn_weight, "shard", axis=1, tiled=True),
        lax.all_gather(mlp_in_weight, "shard", axis=0, tiled=True),
        lax.all_gather(mlp_out_weight, "shard", axis=1, tiled=True),
        lax.all_gather(attn_gain, "shard", axis=0, tiled=True),
        lax.all_gather(mlp_gain, "shard", axis=0, tiled=True),
    )
    qkv_full, attn_full, mlp_in_full, mlp_out_full, attn_gain_low, mlp_gain_low = gathered
    gain_attn = attn_gain_low.astype(jnp.float32)
    gain_mlp = mlp_gain_low.astype(jnp.float32)
    seq_in = inputs[0].astype(jnp.float32)
    batch_count = seq_in.shape[0]
    local_len = seq_in.shape[1]
    tp_width = qkv_full.shape[2]
    local_heads = tp_width // HD
    ext_len = local_len + 2 * HALF
    scaling = 1.0 / math.sqrt(HD)
    query_tile = min(512, local_len)
    tile_count = local_len // query_tile
    key_span = query_tile + 2 * HALF
    ctx_index = lax.axis_index("ctx")
    positions = ctx_index * local_len + jnp.arange(local_len, dtype=jnp.int32)
    seq_lengths = lengths[0]
    valid_rows = (positions[None, :] < seq_lengths[:, None]).astype(jnp.float32)[:, :, None]
    tile_starts = jnp.arange(tile_count, dtype=jnp.int32) * query_tile
    query_pos = (
        ctx_index * local_len
        + tile_starts[:, None]
        + jnp.arange(query_tile, dtype=jnp.int32)[None, :]
    )
    key_pos = (
        ctx_index * local_len
        - HALF
        + tile_starts[:, None]
        + jnp.arange(key_span, dtype=jnp.int32)[None, :]
    )
    distance = query_pos[:, :, None] - key_pos[:, None, :]
    near_keys = (jnp.abs(distance) <= HALF) & (key_pos[:, None, :] >= 0)
    live_keys = (key_pos[None, :, None, :] < seq_lengths[:, None, None, None]) | (distance == 0)[
        None
    ]
    allowed = (near_keys[None] & live_keys)[:, :, None]
    cosine, sine_table = rope_tables(positions.astype(jnp.float32))

    def key_tiles(extended):
        return jnp.stack(
            [
                extended[:, index * query_tile : index * query_tile + key_span]
                for index in range(tile_count)
            ],
            axis=1,
        )

    def untile(tiles):
        total = jnp.zeros((batch_count, ext_len, local_heads, HD), jnp.float32)
        for index in range(tile_count):
            after = ext_len - index * query_tile - key_span
            total = total + jnp.pad(
                tiles[:, index], ((0, 0), (index * query_tile, after), (0, 0), (0, 0))
            )
        return total

    normed_attn, back_norm_attn = jax.vjp(layer_norm, seq_in, gain_attn)
    normed_low = normed_attn.astype(jnp.bfloat16)
    qkv_raw = jnp.einsum("mtd,dcf->mtcf", normed_low, qkv_full, preferred_element_type=jnp.float32)
    heads_raw = qkv_raw.reshape(batch_count, local_len, 3, local_heads, HD)

    def rope_pair(query_raw, key_raw):
        return (rotate(query_raw, cosine, sine_table), rotate(key_raw, cosine, sine_table))

    (query_rot, key_rot), back_rope = jax.vjp(rope_pair, heads_raw[:, :, 0], heads_raw[:, :, 1])
    queries = query_rot.astype(jnp.bfloat16)
    key_value = jnp.stack([key_rot.astype(jnp.bfloat16), heads_raw[:, :, 2].astype(jnp.bfloat16)])
    key_value = key_value.reshape(2, batch_count, local_len, tp_width)
    key_value_ext = padded(key_value, (("ctx", 2),), HALF)
    key_value_ext = key_value_ext.reshape(2, batch_count, ext_len, local_heads, HD)
    keys_tiled = key_tiles(key_value_ext[0])
    values_tiled = key_tiles(key_value_ext[1])
    queries_tiled = queries.reshape(batch_count, tile_count, query_tile, local_heads, HD)

    def masked_scores():
        raw_scores = (
            jnp.einsum(
                "mnqhd,mnkhd->mnhqk", queries_tiled, keys_tiled, preferred_element_type=jnp.float32
            )
            * scaling
        )
        return jnp.where(allowed, raw_scores, masked_score)

    scores = masked_scores()
    top_score = jnp.max(scores, axis=-1, keepdims=True)
    exponent_terms = jnp.exp(scores - top_score)
    denominator = jnp.sum(exponent_terms, axis=-1, keepdims=True)
    soft_low = (exponent_terms / denominator).astype(jnp.bfloat16)
    log_total = top_score + jnp.log(denominator)
    context = jnp.einsum(
        "mnhqk,mnkhd->mnqhd", soft_low, values_tiled, preferred_element_type=jnp.float32
    )
    context_low = context.astype(jnp.bfloat16).reshape(batch_count, local_len, tp_width)
    attn_part = jnp.einsum(
        "mtf,fd->mtd", context_low, attn_full, preferred_element_type=jnp.float32
    )
    attn_out = lax.psum(attn_part, "tp")
    middle = seq_in + attn_out
    normed_mlp, back_norm_mlp = jax.vjp(layer_norm, middle, gain_mlp)
    normed_mlp_low = normed_mlp.astype(jnp.bfloat16)
    gate_up = jnp.einsum(
        "mtd,dcf->mtcf", normed_mlp_low, mlp_in_full, preferred_element_type=jnp.float32
    )
    hidden, back_glu = jax.vjp(geglu, gate_up)
    hidden_low = hidden.astype(jnp.bfloat16)
    mlp_part = jnp.einsum(
        "mtf,fd->mtd", hidden_low, mlp_out_full, preferred_element_type=jnp.float32
    )
    mlp_out = lax.psum(mlp_part.astype(jnp.bfloat16), "tp").astype(jnp.float32)
    layer_out = ((middle + mlp_out) * valid_rows).astype(jnp.bfloat16)[None]
    grad_out = cotangent[0].astype(jnp.float32) * valid_rows
    grad_out_low = grad_out.astype(jnp.bfloat16)
    mlp_out_grad = jnp.einsum(
        "mtf,mtd->fd", hidden_low, grad_out_low, preferred_element_type=jnp.float32
    )
    grad_hidden = jnp.einsum(
        "mtd,fd->mtf", grad_out_low, mlp_out_full, preferred_element_type=jnp.float32
    )
    (grad_gate_up,) = back_glu(grad_hidden)
    grad_gate_low = grad_gate_up.astype(jnp.bfloat16)
    mlp_in_grad = jnp.einsum(
        "mtd,mtcf->dcf", normed_mlp_low, grad_gate_low, preferred_element_type=jnp.float32
    )
    grad_mlp_part = jnp.einsum(
        "mtcf,dcf->mtd", grad_gate_low, mlp_in_full, preferred_element_type=jnp.float32
    )
    grad_normed_mlp = lax.psum(grad_mlp_part, "tp")
    grad_mid_norm, mlp_gain_grad = back_norm_mlp(grad_normed_mlp)
    grad_middle = grad_out + grad_mid_norm
    grad_middle_low = grad_middle.astype(jnp.bfloat16)
    attn_grad = jnp.einsum(
        "mtf,mtd->fd", context_low, grad_middle_low, preferred_element_type=jnp.float32
    )
    grad_context = jnp.einsum(
        "mtd,fd->mtf", grad_middle_low, attn_full, preferred_element_type=jnp.float32
    )
    grad_context = grad_context.astype(jnp.bfloat16).reshape(
        batch_count, tile_count, query_tile, local_heads, HD
    )
    soft_again = jnp.exp(masked_scores() - log_total)
    soft_again_low = soft_again.astype(jnp.bfloat16)
    grad_values = jnp.einsum(
        "mnhqk,mnqhd->mnkhd", soft_again_low, grad_context, preferred_element_type=jnp.float32
    )
    grad_soft = jnp.einsum(
        "mnqhd,mnkhd->mnhqk", grad_context, values_tiled, preferred_element_type=jnp.float32
    )
    row_terms = jnp.sum(soft_again * grad_soft, axis=-1, keepdims=True)
    grad_scores = (soft_again * (grad_soft - row_terms)).astype(jnp.bfloat16)
    grad_queries = (
        jnp.einsum(
            "mnhqk,mnkhd->mnqhd", grad_scores, keys_tiled, preferred_element_type=jnp.float32
        )
        * scaling
    )
    grad_queries = grad_queries.reshape(batch_count, local_len, local_heads, HD)
    grad_keys = (
        jnp.einsum(
            "mnhqk,mnqhd->mnkhd", grad_scores, queries_tiled, preferred_element_type=jnp.float32
        )
        * scaling
    )
    grad_ext = jnp.stack([untile(grad_keys), untile(grad_values)]).reshape(
        2, batch_count, ext_len, tp_width
    )
    rim_pairs = jnp.concatenate([grad_ext[:, :, :HALF], grad_ext[:, :, ext_len - HALF :]], axis=2)
    arrived = padded(rim_pairs, (("ctx", 2),), HALF)
    from_lower = arrived[:, :, :HALF]
    from_upper = arrived[:, :, arrived.shape[2] - HALF :]
    grad_own = grad_ext[:, :, HALF : HALF + local_len]
    grad_own = grad_own + jnp.pad(from_lower, ((0, 0), (0, 0), (0, local_len - HALF), (0, 0)))
    grad_own = grad_own + jnp.pad(from_upper, ((0, 0), (0, 0), (local_len - HALF, 0), (0, 0)))
    grad_key_rot = grad_own[0].reshape(batch_count, local_len, local_heads, HD)
    grad_value_own = grad_own[1].reshape(batch_count, local_len, local_heads, HD)
    grad_query_raw, grad_key_raw = back_rope((grad_queries, grad_key_rot))
    grad_qkv = jnp.stack([grad_query_raw, grad_key_raw, grad_value_own], axis=2)
    grad_qkv_low = grad_qkv.reshape(batch_count, local_len, 3, tp_width).astype(jnp.bfloat16)
    qkv_grad = jnp.einsum(
        "mtd,mtcf->dcf", normed_low, grad_qkv_low, preferred_element_type=jnp.float32
    )
    grad_attn_part = jnp.einsum(
        "mtcf,dcf->mtd", grad_qkv_low, qkv_full, preferred_element_type=jnp.float32
    )
    grad_normed = lax.psum(grad_attn_part, "tp")
    grad_in_norm, attn_gain_grad = back_norm_attn(grad_normed)
    input_grad = (grad_middle + grad_in_norm).astype(jnp.bfloat16)[None]
    partials = (qkv_grad, attn_grad, mlp_in_grad, mlp_out_grad, attn_gain_grad, mlp_gain_grad)
    summed = lax.psum(
        (partials[0], partials[1], partials[2], partials[3], partials[4], partials[5]), "ctx"
    )
    reduced = (
        lax.psum_scatter(summed[0], "shard", scatter_dimension=0, tiled=True),
        lax.psum_scatter(summed[1], "shard", scatter_dimension=1, tiled=True),
        lax.psum_scatter(summed[2], "shard", scatter_dimension=0, tiled=True),
        lax.psum_scatter(summed[3], "shard", scatter_dimension=1, tiled=True),
        lax.psum_scatter(summed[4], "shard", scatter_dimension=0, tiled=True),
        lax.psum_scatter(summed[5], "shard", scatter_dimension=0, tiled=True),
    )
    gain_share = reduced[4].shape[0] // lax.axis_size("tp")
    gain_start = lax.axis_index("tp") * gain_share
    attn_gain_out = lax.dynamic_slice_in_dim(reduced[4], gain_start, gain_share)
    mlp_gain_out = lax.dynamic_slice_in_dim(reduced[5], gain_start, gain_share)
    return (
        layer_out,
        input_grad,
        reduced[0],
        reduced[1],
        reduced[2],
        reduced[3],
        attn_gain_out,
        mlp_gain_out,
    )


def solution(mesh):
    in_specs = (
        P("shard", None, "ctx", None),
        P("shard", None),
        P("shard"),
        P("shard"),
        P("shard", None, "tp"),
        P("tp", "shard"),
        P("shard", None, "tp"),
        P("tp", "shard"),
        P("shard", None, "ctx", None),
    )
    out_specs = (
        P("shard", None, "ctx", None),
        P("shard", None, "ctx", None),
        P("shard", None, "tp"),
        P("tp", "shard"),
        P("shard", None, "tp"),
        P("tp", "shard"),
        P(("shard", "tp")),
        P(("shard", "tp")),
    )
    return jax.shard_map(
        on_device, mesh=mesh, in_specs=in_specs, out_specs=out_specs, check_vma=False
    )
```

profile of v0, /device:TPU:0, one launch (start us, length us, event | category | flops | bytes accessed | tf_op | source)
XLA Modules:
  0.0 1094.5 jit_solution(6729855262283549967)
XLA Ops:
  8.1 5.3 all-gather
  17.6 11.8 %all_gather.19 = bf16[768,3,192]{0,2,1:T(8,128)(2,1)S(1)} all-gather(bf16[384,3,192]{0,2,1:T(8,128)(2,1)S(1)} %copy-done.45), channel_id=1, replica_groups=mesh['shard'=2,'ctx'=4,'tp'=4] {'shard'}, dimensions={0}, use_global_device_ids=true | all-gather | bytes 1327104 | tf_op jit(solution)/shard_map/all_gather | solution.py:67
  43.7 3.7 collective-permute-start
  60.4 7.3 all_gather.20
  67.7 4.4 concatenate.47
  85.1 5.0 fusion.106
  95.1 4.8 fusion.122
  100.6 4.3 all-gather.1
  104.9 6.9 all_gather.23
  111.8 12.6 %all_gather.22 = bf16[768,2,288]{0,2,1:T(8,128)(2,1)} all-gather(bf16[384,2,288]{0,2,1:T(8,128)(2,1)} %param.15), channel_id=1, replica_groups=mesh['shard'=2,'ctx'=4,'tp'=4] {'shard'}, dimensions={0}, use_global_device_ids=true | all-gather | bytes 1327104 | tf_op jit(solution)/shard_map/all_gather | solution.py:69
  124.5 4.5 fusion.37
  129.1 194.1 %all-reduce.23.cloned.1.call-done = f32[2,1024,768]{2,1,0:T(8,128)} async-done(((f32[2,1024,768]{2,1,0:T(8,128)}), f32[2,1024,768]{2,1,0:T(8,128)}) %all-reduce.23.cloned.1.call-update) | async-done | bytes 6291472 | tf_op jit(solution)/shard_map/psum | solution.py:169
  332.0 5.1 multiply_bitcast_fusion
  339.8 4.6 convolution_bitcast_fusion.1
  345.3 6.4 convolution_convert_fusion
  353.6 9.3 fusion.103
  363.9 7.7 fusion.96
  371.7 194.6 %all-reduce.27.cloned.1.call-done = f32[2,1024,768]{2,1,0:T(8,128)} async-done(((f32[2,1024,768]{2,1,0:T(8,128)}), f32[2,1024,768]{2,1,0:T(8,128)}) %all-reduce.27.cloned.1.call-update) | async-done | bytes 6291472 | tf_op jit(solution)/shard_map/psum | solution.py:199
  566.3 6.2 multiply_reduce_fusion.1
  572.5 116.8 %all-reduce.25.cloned.1.call-done = bf16[2,1024,768]{2,1,0:T(8,128)(2,1)} async-done(((bf16[2,1024,768]{2,1,0:T(8,128)(2,1)}), bf16[2,1024,768]{2,1,0:T(8,128)(2,1)}) %all-reduce.25.cloned.1.call-update) | async-done | bytes 3145744 | tf_op jit(solution)/shard_map/psum | solution.py:181
  689.3 8.3 fusion.174
  707.5 14.0 %multiply_reduce_fusion = (f32[2,2,3,512]{3,2,1,0:T(4,128)S(1)}, f32[2,2,3,512,640]{4,3,2,1,0:T(8,128)}) fusion(f32[2,2,3,512,640]{4,3,2,1,0:T(8,128)} %copy-done, f32[2,2,3,512]{3,2,1,0:T(4,128)S(1)} %log_add_fusion, bf16[2,1,640,3,64]{2,4,3,1,0:T(8,128)(2,1)} %copy-done.33, bf16[2,1,640,3,64]{2,4,3,1,0:T(8,128)(2,1)} %copy-done.32, ...), kind=kOutput, calls=%fused_computation.1 | convolution fusion | flops 515598336 | bytes 33275904 | tf_op jit(solution)/shard_map/mnqhd,mnkhd->mnhqk/dot_general | solution.py:217
  722.7 7.4 multiply_convert_fusion
  734.0 4.3 fusion.89
  761.0 7.3 convolution_bitcast_fusion
  770.3 25.6 %reduce-scatter.5.cloned.1.call-done = f32[384,3,192]{0,2,1:T(8,128)} async-done(((f32[768,3,192]{0,2,1:T(8,128)}), f32[384,3,192]{0,2,1:T(8,128)}) %reduce-scatter.5.cloned.1.call-update) | async-done | bytes 884752 | tf_op jit(solution)/shard_map/reduce_scatter | solution.py:264
  795.9 225.4 %all-reduce.29.cloned.1.call-done = f32[2,1024,768]{2,1,0:T(8,128)} async-done(((f32[2,1024,768]{2,1,0:T(8,128)}), f32[2,1024,768]{2,1,0:T(8,128)}) %all-reduce.29.cloned.1.call-update) | async-done | bytes 6291472 | tf_op jit(solution)/shard_map/psum | solution.py:256
  1021.2 4.0 fusion.21
  1029.1 5.0 all-reduce.16
  1034.2 6.7 all-reduce.14
  1042.1 9.2 fusion.30
  1051.3 30.6 %all-reduce.31.cloned.1.call-done = (f32[384,3,192]{0,2,1:T(8,128)}, f32[192,384]{1,0:T(8,128)}, f32[384,2,288]{0,2,1:T(8,128)}, f32[288,384]{1,0:T(8,128)}) async-done(((f32[384,3,192]{0,2,1:T(8,128)}, f32[192,384]{1,0:T(8,128)}, f32[384,2,288]{0,2,1:T(8,128)}, f32[288,384]{1,0:T(8,128)}), (f32[384,3,192]{0,2,1:T(8,128)}, f32[192,384]{1,0:T(8,128)}, f32[384,2,288]{0,2,1:T(8,128)}, ...) | async-done | bytes 2506768 | tf_op jit(solution)/shard_map/psum | solution.py:260
  (246 shorter events, 115.4 us)
Async XLA Ops:
  7.2 8.7 copy-start.1
  7.2 316.0 %all-reduce.23.cloned.1.call-start = ((), (), s32[]{:S(2)}) async-start(), calls=%async_computation.4 | async-start | bytes 12582912 | tf_op jit(solution)/shard_map/psum | solution.py:169
  13.4 15.9 %copy-start.54 = (f32[768]{0:T(1024)}, f32[768]{0:T(1024)S(1)}, u32[]{:S(2)}) copy-start(f32[768]{0:T(1024)S(1)} %reshape.411) | copy-start | bytes 9220
  15.9 16.1 %copy-start.46 = (f32[2,1024]{1,0:T(2,128)}, f32[2,1024]{1,0:T(2,128)S(1)}, u32[]{:S(2)}) copy-start(f32[2,1024]{1,0:T(2,128)S(1)} %broadcast_multiply_fusion.5) | copy-start | bytes 24580
  17.6 14.4 %copy-start.52 = (f32[2,1024]{1,0:T(2,128)}, f32[2,1024]{1,0:T(2,128)S(1)}, u32[]{:S(2)}) copy-start(f32[2,1024]{1,0:T(2,128)S(1)} %fusion.130) | copy-start | bytes 24580
  42.4 25.3 %collective-permute-start.1 = (bf16[2,2,64,192]{2,3,1,0:T(8,128)(2,1)}, bf16[2,2,64,192]{2,3,1,0:T(8,128)(2,1)}, u32[]{:S(2)}, u32[]{:S(2)}) collective-permute-start(bf16[2,2,64,192]{2,3,1,0:T(8,128)(2,1)} %get-tuple-element.43), channel_id=1, source_target_pairs={{4,0},{8,4},{12,8},{5,1},{9,5},{13,9},{6,2},{10,6},{14,10},{7,3},{... | collective-permute-start | bytes 294920 | tf_op jit(solution)/shard_map/ppermute | solution.py:24
  43.7 24.0 %collective-permute-start = (bf16[2,2,64,192]{2,3,1,0:T(8,128)(2,1)}, bf16[2,2,64,192]{2,3,1,0:T(8,128)(2,1)}, u32[]{:S(2)}, u32[]{:S(2)}) collective-permute-start(bf16[2,2,64,192]{2,3,1,0:T(8,128)(2,1)} %get-tuple-element.44), channel_id=1, source_target_pairs={{0,4},{4,8},{8,12},{1,5},{5,9},{9,13},{2,6},{6,10},{10,14},{3,7},{... | collective-permute-start | bytes 294920 | tf_op jit(solution)/shard_map/ppermute | solution.py:22
  73.8 5.9 copy-start.28
  73.8 5.9 copy-start.30
  73.9 8.9 copy-start.32
  74.0 8.9 copy-start.33
  79.7 5.4 copy-start
  82.8 7.3 copy-start.49
  99.9 466.4 %all-reduce.27.cloned.1.call-start = ((), (), s32[]{:S(2)}) async-start(), calls=%async_computation.6 | async-start | bytes 12582912 | tf_op jit(solution)/shard_map/psum | solution.py:199
  111.8 12.7 %copy-start.34 = (bf16[288,768]{1,0:T(8,128)(2,1)}, bf16[288,768]{1,0:T(8,128)(2,1)S(1)}, u32[]{:S(2)}) copy-start(bf16[288,768]{1,0:T(8,128)(2,1)S(1)} %all_gather.23) | copy-start | bytes 1327108
  332.0 5.2 copy-start.6
  344.4 345.0 %all-reduce.25.cloned.1.call-start = ((), (), s32[]{:S(2)}) async-start(), calls=%async_computation.5 | async-start | bytes 6291456 | tf_op jit(solution)/shard_map/psum | solution.py:181
  351.7 418.5 %reduce-scatter.11.cloned.1.call-start = ((), (), s32[]{:S(2)}) async-start(), calls=%async_computation.11 | async-start | bytes 1327104 | tf_op jit(solution)/shard_map/reduce_scatter | solution.py:267
  362.9 407.3 %reduce-scatter.9.cloned.1.call-start = ((), (), s32[]{:S(2)}) async-start(), calls=%async_computation.10 | async-start | bytes 2654208 | tf_op jit(solution)/shard_map/reduce_scatter | solution.py:266
  371.7 398.6 %reduce-scatter.7.cloned.1.call-start = ((), (), s32[]{:S(2)}) async-start(), calls=%async_computation.9 | async-start | bytes 884736 | tf_op jit(solution)/shard_map/reduce_scatter | solution.py:265
  704.1 17.4 %slice-start = ((s8[15728640]{0:T(1024)(128)(4,1)}), s8[3145728]{0:T(1024)(128)(4,1)S(1)}, s32[]{:S(2)}) async-start(s8[15728640]{0:T(1024)(128)(4,1)} %bitcast.348), calls=%async_computation.13 | async-start | bytes 6291456
  707.5 14.0 %slice-start.1 = ((s8[15728640]{0:T(1024)(128)(4,1)}), s8[4194304]{0:T(1024)(128)(4,1)S(1)}, s32[]{:S(2)}) async-start(s8[15728640]{0:T(1024)(128)(4,1)} %bitcast.348), calls=%async_computation.14 | async-start | bytes 8388608
  707.5 14.0 %slice-start.2 = ((s8[15728640]{0:T(1024)(128)(4,1)}), s8[4194304]{0:T(1024)(128)(4,1)S(1)}, s32[]{:S(2)}) async-start(s8[15728640]{0:T(1024)(128)(4,1)} %bitcast.348), calls=%async_computation.15 | async-start | bytes 8388608
  707.5 15.2 %slice-start.3 = ((s8[15728640]{0:T(1024)(128)(4,1)}), s8[4194304]{0:T(1024)(128)(4,1)S(1)}, s32[]{:S(2)}) async-start(s8[15728640]{0:T(1024)(128)(4,1)} %bitcast.348), calls=%async_computation.16 | async-start | bytes 8388608
  722.7 7.4 copy-start.29
  722.7 7.4 copy-start.31
  743.0 5.6 collective-permute-start.2
  745.6 4.5 collective-permute-start.3
  748.5 47.3 %reduce-scatter.5.cloned.1.call-start = ((), (), s32[]{:S(2)}) async-start(), calls=%async_computation.8 | async-start | bytes 2654208 | tf_op jit(solution)/shard_map/reduce_scatter | solution.py:264
  760.9 260.3 %all-reduce.29.cloned.1.call-start = ((), (), s32[]{:S(2)}) async-start(), calls=%async_computation.7 | async-start | bytes 12582912 | tf_op jit(solution)/shard_map/psum | solution.py:256
  768.3 313.6 %all-reduce.31.cloned.1.call-start = ((), (), s32[]{:S(2)}) async-start(), calls=%async_computation.12 | async-start | bytes 5013504 | tf_op jit(solution)/shard_map/psum | solution.py:260
  795.9 229.3 %copy-start.51 = (f32[2,1024]{1,0:T(2,128)S(1)}, f32[2,1024]{1,0:T(2,128)}, u32[]{:S(2)}) copy-start(f32[2,1024]{1,0:T(2,128)} %copy-done.50) | copy-start | bytes 24580
  (45 other events, 94.3 us)
Sparse Core Ops, SparseCore 0:
  100.0 223.1 all-reduce.22
  344.5 221.7 all-reduce.26
  569.3 120.0 all-reduce.24
  692.0 17.5 reduce-scatter.10
  711.7 28.2 reduce-scatter.8
  748.6 16.0 reduce-scatter.6
  767.6 28.2 reduce-scatter.4
  798.3 222.8 all-reduce.28
  1024.0 57.8 all-reduce.30
where the time goes:
time: 1100 us; the launch traced here: 1090 us
  waiting for transfers between devices  789 us (72%)
  matrix products  88.2 us (8%)
  other arithmetic  76 us (7%)
  blocking collectives  60 us (5%)
  local copies, waits for them, and re-layouts  56.3 us (5%)
  between operations  15.9 us (1%)
    psum x1, waiting for transfers between devices, on_device(): grad_normed = lax.psum(grad_attn_part, 'tp')  225 us
    psum x1, waiting for transfers between devices, on_device(): grad_normed_mlp = lax.psum(grad_mlp_part, 'tp')  195 us
    psum x1, waiting for transfers between devices, on_device(): attn_out = lax.psum(attn_part, 'tp')  194 us
    psum x1, waiting for transfers between devices, on_device(): mlp_out = lax.psum(mlp_part.astype(jnp.bfloat16), 'tp').astype(jnp.float32)  117 us
    psum x1, waiting for transfers between devices, on_device(): lax.psum((partials[0], partials[1], partials[2], partials[3], partials[4]...  30.6 us
    unnamed x137, local copies, waits for them, and re-layouts  29.4 us
    reduce_scatter x1, waiting for transfers between devices, on_device(): lax.psum_scatter(summed[0], 'shard', scatter_dimension=0, tiled=True)  25.6 us
  transfers between devices with their start and end apart: 13, of which 7 were waited for; matrix products, arithmetic and copies ran while one was open for 12% of the time, Pallas kernels for 0%

commit v1 on v0

--- a/solution.py
+++ b/solution.py
@@ -1,3 +1,4 @@
+import functools
 import math
 import jax
 import jax.numpy as jnp
@@ -9,6 +10,23 @@
 norm_eps = 1e-05
 rope_base = 10000.0
 masked_score = -1e30
+
+
+def pair_streams(chunk, axis_id):
+    p_count = lax.axis_size(axis_id)
+
+    def _process_block(all_rows, part_now):
+        if part_now >= p_count:
+            return all_rows
+        carry = lax.ppermute(
+            all_rows, axis_id, [(dev_j, dev_j ^ part_now) for dev_j in range(p_count)]
+        )
+        return _process_block(all_rows + carry, 2 * part_now)
+
+    return _process_block(chunk, 1)
+
+
+routes_all_check = functools.partial(pair_streams, axis_id="tp")
 
 
 def padded(cells, sides, width):
@@ -166,7 +184,7 @@
     attn_part = jnp.einsum(
         "mtf,fd->mtd", context_low, attn_full, preferred_element_type=jnp.float32
     )
-    attn_out = lax.psum(attn_part, "tp")
+    attn_out = routes_all_check(attn_part)
     middle = seq_in + attn_out
     normed_mlp, back_norm_mlp = jax.vjp(layer_norm, middle, gain_mlp)
     normed_mlp_low = normed_mlp.astype(jnp.bfloat16)

time: 1100 us -> 1270 us (1.15)
  waiting for transfers between devices: 789 us -> 936 us
  local copies, waits for them, and re-layouts: 56.3 us -> 73.3 us
    ppermute x0 -> x2, waiting for transfers between devices: none -> 376 us  [_process_block(): lax.ppermute(all_rows, axis_id, [(dev_j, dev_j ^ part_now) for dev_j in r...]
    psum x1 -> x0, waiting for transfers between devices: 194 us -> none  [on_device(): attn_out = lax.psum(attn_part, 'tp')]
    psum x1, waiting for transfers between devices: 225 us -> 199 us  [on_device(): grad_normed = lax.psum(grad_attn_part, 'tp')]
    unnamed x137, local copies, waits for them, and re-layouts: 29.4 us -> 46.4 us
  transfers between devices with their start and end apart: 13 -> 14, of which waited for: 7 -> 8; matrix products, arithmetic and copies ran while one was open for 12% -> 11% of each run, Pallas kernels for 0% -> 0%
where the time goes in v1:
time: 1270 us; the launch traced here: 1260 us
  waiting for transfers between devices  936 us (74%)
  matrix products  82.2 us (6%)
  other arithmetic  80.8 us (6%)
  local copies, waits for them, and re-layouts  73.3 us (6%)
  blocking collectives  59.1 us (5%)
  between operations  17.4 us (1%)
  starting transfers between devices  14.1 us (1%)
    ppermute x2, waiting for transfers between devices, _process_block(): lax.ppermute(all_rows, axis_id, [(dev_j, dev_j ^ part_now) for dev_j in r...  376 us
    psum x1, waiting for transfers between devices, on_device(): grad_normed = lax.psum(grad_attn_part, 'tp')  199 us
    psum x1, waiting for transfers between devices, on_device(): grad_normed_mlp = lax.psum(grad_mlp_part, 'tp')  196 us
    psum x1, waiting for transfers between devices, on_device(): mlp_out = lax.psum(mlp_part.astype(jnp.bfloat16), 'tp').astype(jnp.float32)  117 us
    unnamed x137, local copies, waits for them, and re-layouts  46.4 us
    psum x1, waiting for transfers between devices, on_device(): lax.psum((partials[0], partials[1], partials[2], partials[3], partials[4]...  26.4 us
  transfers between devices with their start and end apart: 14, of which 8 were waited for; matrix products, arithmetic and copies ran while one was open for 11% of the time, Pallas kernels for 0%

profile of v1, /device:TPU:0, one launch (start us, length us, event | category | flops | bytes accessed | tf_op | source)
XLA Modules:
  0.0 1262.8 jit_solution(16985900919278733898)
XLA Ops:
  8.7 5.2 all-gather
  14.0 13.8 %all_gather.19 = bf16[768,3,192]{0,2,1:T(8,128)(2,1)} all-gather(bf16[384,3,192]{0,2,1:T(8,128)(2,1)} %param.13), channel_id=1, replica_groups=mesh['shard'=2,'ctx'=4,'tp'=4] {'shard'}, dimensions={0}, use_global_device_ids=true | all-gather | bytes 1327104 | tf_op jit(solution)/shard_map/all_gather | solution.py:85
  64.5 7.1 all_gather.20
  71.5 4.4 concatenate.47
  88.9 5.0 fusion.105
  102.7 135.6 %collective-permute-done.2 = f32[2,1024,768]{1,2,0:T(8,128)S(1)} collective-permute-done((f32[2,1024,768]{1,2,0:T(8,128)S(1)}, f32[2,1024,768]{1,2,0:T(8,128)S(1)}, u32[]{:S(2)}, u32[]{:S(2)}) %collective-permute-start.2) | collective-permute-done | bytes 6291488 | tf_op jit(solution)/shard_map/ppermute | solution.py:21
  245.0 4.3 all-gather.1
  249.3 4.6 copy.89
  254.0 6.8 all_gather.23
  260.8 10.2 all_gather.22
  274.1 240.6 %collective-permute-done.3 = f32[2,1024,768]{1,2,0:T(8,128)} collective-permute-done((f32[2,1024,768]{1,2,0:T(8,128)}, f32[2,1024,768]{1,2,0:T(8,128)}, u32[]{:S(2)}, u32[]{:S(2)}) %collective-permute-start.3) | collective-permute-done | bytes 6291488 | tf_op jit(solution)/shard_map/ppermute | solution.py:21
  514.7 7.1 fusion.176
  526.8 5.1 multiply_bitcast_fusion
  534.5 4.6 convolution_bitcast_fusion.1
  540.1 5.9 convolution_convert_fusion
  547.9 9.0 fusion.102
  557.8 7.5 fusion.95
  565.5 195.9 %all-reduce.24.cloned.1.call-done = f32[2,1024,768]{1,2,0:T(8,128)} async-done(((f32[2,1024,768]{1,2,0:T(8,128)}), f32[2,1024,768]{1,2,0:T(8,128)}) %all-reduce.24.cloned.1.call-update) | async-done | bytes 6291472 | tf_op jit(solution)/shard_map/psum | solution.py:217
  761.4 6.3 multiply_reduce_fusion.1
  767.7 116.7 %all-reduce.22.cloned.1.call-done = bf16[2,1024,768]{1,2,0:T(8,128)(2,1)} async-done(((bf16[2,1024,768]{1,2,0:T(8,128)(2,1)}), bf16[2,1024,768]{1,2,0:T(8,128)(2,1)}) %all-reduce.22.cloned.1.call-update) | async-done | bytes 3145744 | tf_op jit(solution)/shard_map/psum | solution.py:199
  884.4 8.0 fusion.174
  901.9 13.9 %multiply_reduce_fusion = (f32[2,2,3,512]{3,2,1,0:T(4,128)S(1)}, f32[2,2,3,512,640]{4,3,2,1,0:T(8,128)}) fusion(f32[2,2,3,512,640]{4,3,2,1,0:T(8,128)} %copy-done, f32[2,2,3,512]{3,2,1,0:T(4,128)S(1)} %log_add_fusion, bf16[2,1,640,3,64]{2,4,3,1,0:T(8,128)(2,1)} %copy-done.32, bf16[2,1,640,3,64]{2,4,3,1,0:T(8,128)(2,1)} %copy-done.31, ...), kind=kOutput, calls=%fused_computation.1 | convolution fusion | flops 515598336 | bytes 33275904 | tf_op jit(solution)/shard_map/mnqhd,mnkhd->mnhqk/dot_general | solution.py:235
  917.0 7.4 multiply_convert_fusion
  955.2 7.3 convolution_bitcast_fusion
  964.3 5.1 copy.105
  969.5 20.3 %reduce-scatter.5.cloned.1.call-done = f32[384,3,192]{0,2,1:T(8,128)} async-done(((f32[768,3,192]{0,2,1:T(8,128)}), f32[384,3,192]{0,2,1:T(8,128)}) %reduce-scatter.5.cloned.1.call-update) | async-done | bytes 884752 | tf_op jit(solution)/shard_map/reduce_scatter | solution.py:282
  989.8 199.2 %all-reduce.26.cloned.1.call-done = f32[2,1024,768]{1,2,0:T(8,128)} async-done(((f32[2,1024,768]{1,2,0:T(8,128)}), f32[2,1024,768]{1,2,0:T(8,128)}) %all-reduce.26.cloned.1.call-update) | async-done | bytes 6291472 | tf_op jit(solution)/shard_map/psum | solution.py:274
  1196.9 5.0 all-reduce.16
  1202.1 6.7 all-reduce.14
  1210.0 8.5 fusion.30
  1218.5 4.6 copy.106
  1223.1 26.4 %all-reduce.28.cloned.1.call-done = (f32[384,3,192]{0,2,1:T(8,128)}, f32[192,384]{1,0:T(8,128)}, f32[384,2,288]{0,2,1:T(8,128)}, f32[288,384]{1,0:T(8,128)}) async-done(((f32[384,3,192]{0,2,1:T(8,128)}, f32[192,384]{1,0:T(8,128)}, f32[384,2,288]{0,2,1:T(8,128)}, f32[288,384]{1,0:T(8,128)}), (f32[384,3,192]{0,2,1:T(8,128)}, f32[192,384]{1,0:T(8,128)}, f32[384,2,288]{0,2,1:T(8,128)}, ...) | async-done | bytes 2506768 | tf_op jit(solution)/shard_map/psum | solution.py:278
  (248 shorter events, 137.3 us)
Async XLA Ops:
  8.0 753.4 %all-reduce.24.cloned.1.call-start = ((), (), s32[]{:S(2)}) async-start(), calls=%async_computation.5 | async-start | bytes 12582912 | tf_op jit(solution)/shard_map/psum | solution.py:217
  14.0 18.5 %copy-start.52 = (f32[768]{0:T(1024)}, f32[768]{0:T(1024)S(1)}, u32[]{:S(2)}) copy-start(f32[768]{0:T(1024)S(1)} %reshape.411) | copy-start | bytes 9220
  31.0 483.7 %copy-start.1 = (bf16[1,2,1024,768]{2,3,1,0:T(8,128)(2,1)}, bf16[1,2,1024,768]{2,3,1,0:T(8,128)(2,1)S(1)}, u32[]{:S(2)}) copy-start(bf16[1,2,1024,768]{2,3,1,0:T(8,128)(2,1)S(1)} %copy.77) | copy-start | bytes 9437188
  46.0 25.5 %collective-permute-start.1 = (bf16[2,2,64,192]{2,3,1,0:T(8,128)(2,1)}, bf16[2,2,64,192]{2,3,1,0:T(8,128)(2,1)}, u32[]{:S(2)}, u32[]{:S(2)}) collective-permute-start(bf16[2,2,64,192]{2,3,1,0:T(8,128)(2,1)} %get-tuple-element.67), channel_id=1, source_target_pairs={{4,0},{8,4},{12,8},{5,1},{9,5},{13,9},{6,2},{10,6},{14,10},{7,3},{... | collective-permute-start | bytes 294920 | tf_op jit(solution)/shard_map/ppermute | solution.py:42
  47.3 24.3 %collective-permute-start = (bf16[2,2,64,192]{2,3,1,0:T(8,128)(2,1)}, bf16[2,2,64,192]{2,3,1,0:T(8,128)(2,1)}, u32[]{:S(2)}, u32[]{:S(2)}) collective-permute-start(bf16[2,2,64,192]{2,3,1,0:T(8,128)(2,1)} %get-tuple-element.68), channel_id=1, source_target_pairs={{0,4},{4,8},{8,12},{1,5},{5,9},{9,13},{2,6},{6,10},{10,14},{3,7},{... | collective-permute-start | bytes 294920 | tf_op jit(solution)/shard_map/ppermute | solution.py:40
  77.6 5.9 copy-start.27
  77.6 5.9 copy-start.29
  77.8 8.9 copy-start.31
  77.8 8.9 copy-start.32
  83.5 5.4 copy-start
  86.7 7.3 copy-start.47
  101.1 143.9 %copy-start.56 = (bf16[384]{0:T(512)(128)(2,1)S(1)}, bf16[384]{0:T(512)(128)(2,1)}, u32[]{:S(2)}) copy-start(bf16[384]{0:T(512)(128)(2,1)} %param.12) | copy-start | bytes 2308
  101.1 137.2 %collective-permute-start.2 = (f32[2,1024,768]{1,2,0:T(8,128)S(1)}, f32[2,1024,768]{1,2,0:T(8,128)S(1)}, u32[]{:S(2)}, u32[]{:S(2)}) collective-permute-start(f32[2,1024,768]{1,2,0:T(8,128)S(1)} %fusion.122), channel_id=1, source_target_pairs={{0,1},{1,0},{2,3},{3,2},{4,5},{5,4},{6,7},{7,6},{8,9},{9,8},{10,11... | collective-permute-start | bytes 18874376 | tf_op jit(solution)/shard_map/ppermute | solution.py:21
  242.4 272.3 %collective-permute-start.3 = (f32[2,1024,768]{1,2,0:T(8,128)}, f32[2,1024,768]{1,2,0:T(8,128)}, u32[]{:S(2)}, u32[]{:S(2)}) collective-permute-start(f32[2,1024,768]{1,2,0:T(8,128)} %add.232), channel_id=1, source_target_pairs={{0,2},{1,3},{2,0},{3,1},{4,6},{5,7},{6,4},{7,5},{8,10},{9,11},{10,... | collective-permute-start | bytes 18874376 | tf_op jit(solution)/shard_map/ppermute | solution.py:21
  260.8 13.3 %copy-start.33 = (bf16[288,768]{1,0:T(8,128)(2,1)}, bf16[288,768]{1,0:T(8,128)(2,1)S(1)}, u32[]{:S(2)}) copy-start(bf16[288,768]{1,0:T(8,128)(2,1)S(1)} %all_gather.23) | copy-start | bytes 1327108
  526.8 5.2 copy-start.6
  539.1 345.3 %all-reduce.22.cloned.1.call-start = ((), (), s32[]{:S(2)}) async-start(), calls=%async_computation.4 | async-start | bytes 6291456 | tf_op jit(solution)/shard_map/psum | solution.py:199
  546.1 423.4 %reduce-scatter.11.cloned.1.call-start = ((), (), s32[]{:S(2)}) async-start(), calls=%async_computation.10 | async-start | bytes 1327104 | tf_op jit(solution)/shard_map/reduce_scatter | solution.py:285
  557.0 412.5 %reduce-scatter.9.cloned.1.call-start = ((), (), s32[]{:S(2)}) async-start(), calls=%async_computation.9 | async-start | bytes 2654208 | tf_op jit(solution)/shard_map/reduce_scatter | solution.py:284
  565.3 404.2 %reduce-scatter.7.cloned.1.call-start = ((), (), s32[]{:S(2)}) async-start(), calls=%async_computation.8 | async-start | bytes 884736 | tf_op jit(solution)/shard_map/reduce_scatter | solution.py:283
  898.5 17.3 %slice-start = ((s8[15728640]{0:T(1024)(128)(4,1)}), s8[3145728]{0:T(1024)(128)(4,1)S(1)}, s32[]{:S(2)}) async-start(s8[15728640]{0:T(1024)(128)(4,1)} %bitcast.348), calls=%async_computation.12 | async-start | bytes 6291456
  901.9 13.9 %slice-start.1 = ((s8[15728640]{0:T(1024)(128)(4,1)}), s8[4194304]{0:T(1024)(128)(4,1)S(1)}, s32[]{:S(2)}) async-start(s8[15728640]{0:T(1024)(128)(4,1)} %bitcast.348), calls=%async_computation.13 | async-start | bytes 8388608
  901.9 13.9 %slice-start.2 = ((s8[15728640]{0:T(1024)(128)(4,1)}), s8[4194304]{0:T(1024)(128)(4,1)S(1)}, s32[]{:S(2)}) async-start(s8[15728640]{0:T(1024)(128)(4,1)} %bitcast.348), calls=%async_computation.14 | async-start | bytes 8388608
  901.9 15.1 %slice-start.3 = ((s8[15728640]{0:T(1024)(128)(4,1)}), s8[4194304]{0:T(1024)(128)(4,1)S(1)}, s32[]{:S(2)}) async-start(s8[15728640]{0:T(1024)(128)(4,1)} %bitcast.348), calls=%async_computation.15 | async-start | bytes 8388608
  917.0 7.4 copy-start.28
  917.0 7.4 copy-start.30
  937.2 6.0 collective-permute-start.4
  939.8 4.5 collective-permute-start.5
  943.2 46.6 %reduce-scatter.5.cloned.1.call-start = ((), (), s32[]{:S(2)}) async-start(), calls=%async_computation.7 | async-start | bytes 2654208 | tf_op jit(solution)/shard_map/reduce_scatter | solution.py:282
  955.1 233.9 %all-reduce.26.cloned.1.call-start = ((), (), s32[]{:S(2)}) async-start(), calls=%async_computation.6 | async-start | bytes 12582912 | tf_op jit(solution)/shard_map/psum | solution.py:274
  962.5 287.0 %all-reduce.28.cloned.1.call-start = ((), (), s32[]{:S(2)}) async-start(), calls=%async_computation.11 | async-start | bytes 5013504 | tf_op jit(solution)/shard_map/psum | solution.py:278
  989.8 203.2 %copy-start.49 = (f32[2,1024]{1,0:T(2,128)S(1)}, f32[2,1024]{1,0:T(2,128)}, u32[]{:S(2)}) copy-start(f32[2,1024]{1,0:T(2,128)} %copy-done.48) | copy-start | bytes 24580
  (44 other events, 97.9 us)
Sparse Core Ops, SparseCore 0:
  539.2 222.0 all-reduce.23
  764.3 120.0 all-reduce.21
  962.6 226.3 all-reduce.25
  1191.6 57.8 all-reduce.27
Sparse Core Ops, SparseCore 1:
  557.0 18.0 reduce-scatter.10
  577.2 28.1 reduce-scatter.8
  943.2 16.0 reduce-scatter.6
  961.6 28.1 reduce-scatter.4
